TPU v7x, 32 devices: a whole 2x2x4 slice. The times are simulated.
32 devices in a mesh: island: 8 (over z, x), fsdp: 4 (over y, core).
Axes of the slice: x: 2, y: 2, z: 4, core: 2. Of those that a mesh axis runs over, the one named last changes fastest.
Arguments:
- local_weights: bfloat16 [8, 4096, 512], P('island', 'fsdp'), may hold values from -6 to 6
- adam_first: bfloat16 [8, 4096, 512], P('island', 'fsdp'), may hold values from -6 to 6
- adam_second: bfloat16 [8, 4096, 512], P('island', 'fsdp'), may hold values from 0.5 to 4
- global_weights: float32 [4096, 512], P('fsdp'), may hold values from -6 to 6
- outer_momentum: float32 [4096, 512], P('fsdp'), may hold values from -3 to 3
- inputs: bfloat16 [8, 512, 4096], P('island', 'fsdp'), may hold values from -6 to 6
- key_cotangent: bfloat16 [8, 512, 512], P('island', 'fsdp'), may hold values from -24 to 24
Outputs:
- new_local: bfloat16 [8, 4096, 512], P('island', 'fsdp')
- new_first: bfloat16 [8, 4096, 512], P('island', 'fsdp')
- new_second: bfloat16 [8, 4096, 512], P('island', 'fsdp')
- new_global: float32 [4096, 512], P('fsdp')
- new_momentum: float32 [4096, 512], P('fsdp')
All inputs are finite; a program needn't handle non-finite values.
Results may differ from a plain program's by a relative error of at most 0.0065.
Values may be sent and summed in bfloat16 or wider, within the bound.
A program may use at most 64 MiB of HBM per device.

v0:
```python
import functools

import jax
import jax.numpy as jnp
from jax import lax
from jax.experimental import pallas as pl
from jax.experimental.pallas import tpu as pltpu
from jax.sharding import PartitionSpec as P

HEAD_DIM = 128
MESH = pl.DeviceIdType.MESH

beta_one = 0.9
beta_two = 0.95
inner_rate = 0.02
weight_decay = 0.1
adam_epsilon = 1e-08
norm_epsilon = 1e-06
outer_rate = 0.7
outer_beta = 0.9
merge_weight = 0.5


def chunk_count(rows, islands):
    for chunks in (8, 4, 2, 1):
        if islands & (islands - 1) == 0 and rows % (islands * chunks * 16) == 0:
            return chunks
    return 0


def head_backward(keys, upstream, scale):
    squares = jnp.mean(keys * keys, axis=-1, keepdims=True)
    inverse = lax.rsqrt(squares + norm_epsilon)
    normed = keys * inverse
    projected = jnp.mean(upstream * normed, axis=-1, keepdims=True)
    return (inverse * (upstream - normed * projected) * scale).astype(jnp.bfloat16)


def exchange(islands, shards, chunks, scale, *refs):
    w_hbm, x_hbm, cot_hbm = refs[:3]
    if chunks:
        (grad, mean, w, x, cot, lsem, wp, xin, xp, psend, precv, kgin, kgp, kg, own,
         ysem, psem, ksem, csem, fsem, landed, part, gathered, hsem) = refs[3:]
    else:
        (grad, w, x, cot, lsem, wp, xin, xp, psend, precv, kgin, kgp, kg, own,
         ysem, psem, ksem, csem, fsem) = refs[3:]
    rows, width = w.shape
    chips = shards // 2
    island = lax.axis_index("island")
    shard = lax.axis_index("fsdp")
    core = lax.rem(shard, 2)
    chip = shard // 2
    partner = (island, chip * 2 + 1 - core)

    def peer(step):
        return (island, lax.rem(chip + step, chips) * 2 + core)

    def back(step):
        return (island, lax.rem(chip + chips - step, chips) * 2 + core)

    targets = [partner] + [peer(step) for step in range(1, chips)]
    if chunks:
        levels = islands.bit_length() - 1
        sides = [lax.rem(island // 2**bit, 2) for bit in range(levels)]
        mates = [(island + (1 - 2 * sides[bit]) * 2**bit, shard) for bit in range(levels)]
        targets += mates

    loads = [
        pltpu.make_async_copy(source, place, lsem.at[index])
        for index, (source, place) in enumerate(((w_hbm, w), (x_hbm, x), (cot_hbm, cot)))
    ]
    for load in loads:
        load.start()

    barrier = pltpu.get_barrier_semaphore()
    for target in targets:
        pl.semaphore_signal(barrier, inc=1, device_id=target, device_id_type=MESH)
    pl.semaphore_wait(barrier, len(targets))

    def remote(src, dst, sems, where, target):
        return pltpu.make_async_remote_copy(
            src_ref=src,
            dst_ref=dst,
            send_sem=sems.at[(0,) + where],
            recv_sem=sems.at[(1,) + where],
            device_id=target,
            device_id_type=MESH,
        )

    def columns(start):
        return pl.ds(pl.multiple_of(start, rows), rows)

    copies = []

    def begin(copy):
        copy.start()
        copies.append(copy)
        return copy

    y1 = []
    for step in range(1, chips):
        there = lax.rem(chip + step, chips)
        y1.append(begin(remote(
            x_hbm.at[:, pl.ds(pl.multiple_of(there * 2 * rows, 2 * rows), 2 * rows)],
            xin.at[step - 1], ysem, (step - 1,), peer(step))))
    halves, returns = {}, {}
    if chunks:
        span = rows // chunks
        orders = [
            [1, 0] + list(range(2, levels)) if levels > 1 and q % 2 == 1 else list(range(levels))
            for q in range(chunks)
        ]
        starts = []
        for q in range(chunks):
            begins = [q * span]
            for level, bit in enumerate(orders[q]):
                begins.append(begins[level] + sides[bit] * (span >> (level + 1)))
            starts.append(begins)

    def segment(q, level):
        return pl.ds(pl.multiple_of(starts[q][level], span >> level), span >> level)

    def landing(level):
        return pl.ds(span - (span >> level), span >> (level + 1))

    def send_half(q, level):
        bit, size = orders[q][level], span >> (level + 1)
        away = starts[q][level] + (1 - sides[bit]) * size
        source = part if level else w_hbm
        halves[q, level] = begin(remote(
            source.at[pl.ds(pl.multiple_of(away, size), size)],
            landed.at[q, landing(level)], hsem, (q, level), mates[bit]))

    def send_back(q, level):
        place = segment(q, level + 1)
        returns[q, level] = begin(remote(
            gathered.at[place], gathered.at[place], hsem, (q, levels + level),
            mates[orders[q][level]]))

    for q in range(chunks):
        send_half(q, 0)
    wcopy = begin(remote(w_hbm, wp, csem, (0,), partner))
    xcopy = [begin(remote(
        x_hbm.at[:, columns((chip * 2 + 1 - core) * rows)], xp.at[0], csem, (1,), partner))]

    def step_of(q, stage):
        if stage < levels:
            halves[q, stage].wait_recv()
            place = segment(q, stage + 1)
            held = (part if stage else w)[place, :].astype(jnp.float32)
            total = held + landed[q, landing(stage), :].astype(jnp.float32)
            if stage + 1 < levels:
                part[place, :] = total.astype(jnp.bfloat16)
                send_half(q, stage + 1)
            else:
                gathered[place, :] = (total / islands).astype(jnp.bfloat16)
                send_back(q, levels - 1)
        else:
            level = 2 * levels - 1 - stage
            returns[q, level].wait_recv()
            if level:
                send_back(q, level - 1)

    def product(left, right):
        return jnp.dot(left, right, preferred_element_type=jnp.float32)

    stages = []
    for q in range(chunks):
        for stage in range(2 * levels):
            late = (q // 2) * 6.0 / chunks
            stages.append((stage + late, q, stage))
    stages.sort()

    def advance(until):
        while stages and stages[0][0] <= until:
            step_of(*stages.pop(0)[1:])

    for load in loads:
        load.wait()
    advance(0.5)
    wcopy.wait_recv()
    own[...] = product(x[:, columns(shard * rows)], w[...]) + product(
        x[:, columns((chip * 2 + 1 - core) * rows)], wp[...])
    advance(3.3)

    y3 = []
    for step in range(1, chips):
        y1[step - 1].wait_recv()
        xcopy.append(begin(remote(
            xin.at[step - 1, :, columns((1 - core) * rows)], xp.at[step], csem, (step + 1,), partner)))
        psend[step - 1] = (product(xin[step - 1, :, columns(core * rows)], w[...]) + product(
            xin[step - 1, :, columns((1 - core) * rows)], wp[...])).astype(jnp.bfloat16)
        y3.append(begin(remote(
            psend.at[step - 1], precv.at[step - 1], psem, (step - 1,), back(step))))
    advance(5.1)

    keys = own[...]
    for step in range(1, chips):
        y3[step - 1].wait_recv()
        keys += precv[step - 1].astype(jnp.float32)
    keys = keys * scale
    for head in range(width // HEAD_DIM):
        lanes = slice(head * HEAD_DIM, (head + 1) * HEAD_DIM)
        kg[:, lanes] = head_backward(keys[:, lanes], cot[:, lanes].astype(jnp.float32), scale)
    y4 = [
        begin(remote(kg, kgin.at[step - 1], ksem, (step - 1,), peer(step)))
        for step in range(1, chips)
    ]
    forwards = [begin(remote(kg, kgp.at[0], fsem, (0,), partner))]

    tile = min(256, rows)

    def add_block(read, upstream, first=False):
        @pl.loop(0, rows // tile)
        def _(t):
            start = pl.multiple_of(t * tile, tile)
            term = lax.dot_general(
                read(start), upstream[...], (((0,), (0,)), ((), ())),
                preferred_element_type=jnp.float32,
            ).astype(jnp.bfloat16).astype(jnp.float32)
            place = pl.ds(start, tile)
            grad[place, :] = term if first else grad[place, :] + term

    def lane(base):
        def at(start):
            return pl.ds(pl.multiple_of(base + start, tile), tile)
        return at

    mine = lane(shard * rows)
    add_block(lambda start: x[:, mine(start)], kg, first=True)
    forwards[0].wait_recv()
    xcopy[0].wait_recv()
    add_block(lambda start: xp[0, :, pl.ds(start, tile)], kgp.at[0])
    advance(6.4)
    inner = lane(core * rows)
    for step in range(1, chips):
        y4[step - 1].wait_recv()
        forwards.append(begin(remote(
            kgin.at[step - 1], kgp.at[step], fsem, (step,), partner)))
        add_block(lambda start: xin[step - 1, :, inner(start)], kgin.at[step - 1])
    advance(6.9)
    for step in range(1, chips):
        xcopy[step].wait_recv()
        forwards[step].wait_recv()
        add_block(lambda start: xp[step, :, pl.ds(start, tile)], kgp.at[step])
    advance(1000)
    if chunks:
        mean[...] = gathered[...]
    for copy in copies:
        copy.wait_send()


def local(
    local_weights, adam_first, adam_second, global_weights, outer_momentum, inputs, key_cotangent
):
    weights = local_weights[0]
    tokens = inputs[0]
    rows, width = weights.shape
    count, depth = tokens.shape
    scale = float(depth) ** (-0.5)
    islands, shards = lax.axis_size("island"), lax.axis_size("fsdp")
    chips = shards // 2
    others = max(chips - 1, 1)
    chunks = chunk_count(rows, islands)
    bf16, f32 = jnp.bfloat16, jnp.float32
    dma = pltpu.SemaphoreType.DMA
    out_shape = [jax.ShapeDtypeStruct((rows, width), f32)]
    scratch = [
        pltpu.VMEM((rows, width), bf16),
        pltpu.VMEM((count, depth), bf16),
        pltpu.VMEM((count, width), bf16),
        dma((3,)),
        pltpu.VMEM((rows, width), bf16),
        pltpu.VMEM((others, count, 2 * rows), bf16),
        pltpu.VMEM((chips, count, rows), bf16),
        pltpu.VMEM((others, count, width), bf16),
        pltpu.VMEM((others, count, width), bf16),
        pltpu.VMEM((others, count, width), bf16),
        pltpu.VMEM((chips, count, width), bf16),
        pltpu.VMEM((count, width), bf16),
        pltpu.VMEM((count, width), f32),
        dma((2, others)),
        dma((2, others)),
        dma((2, others)),
        dma((2, chips + 1)),
        dma((2, chips)),
    ]
    if chunks:
        levels = islands.bit_length() - 1
        out_shape.append(jax.ShapeDtypeStruct((rows, width), bf16))
        scratch += [
            pltpu.VMEM((chunks, rows // chunks, width), bf16),
            pltpu.VMEM((rows, width), bf16),
            pltpu.VMEM((rows, width), bf16),
            dma((2, chunks, 2 * levels)),
        ]
    vmem = pl.BlockSpec(memory_space=pltpu.VMEM)
    results = pl.pallas_call(
        functools.partial(exchange, islands, shards, chunks, scale),
        out_shape=out_shape,
        in_specs=[pl.BlockSpec(memory_space=pltpu.HBM)] * 3,
        out_specs=[vmem] * len(out_shape),
        scratch_shapes=scratch,
        compiler_params=pltpu.CompilerParams(
            collective_id=0, has_side_effects=True, vmem_limit_bytes=40 * 1024 * 1024
        ),
    )(*(pltpu.with_memory_space_constraint(a, pltpu.HBM) for a in (weights, tokens, key_cotangent[0])))
    gradient = results[0]
    if chunks:
        mean_local = results[1].astype(jnp.float32)
    else:
        mean_local = lax.psum(weights.astype(jnp.float32), "island") / islands
    outer_grad = global_weights - mean_local
    new_momentum = outer_beta * outer_momentum + outer_grad
    new_global = global_weights - outer_rate * (outer_grad + outer_beta * new_momentum)
    first_new = beta_one * adam_first[0].astype(jnp.float32) + (1.0 - beta_one) * gradient
    second_new = (
        beta_two * adam_second[0].astype(jnp.float32) + (1.0 - beta_two) * gradient * gradient
    )
    current = weights.astype(jnp.float32)
    inner = current - inner_rate * (
        first_new / (jnp.sqrt(second_new) + adam_epsilon) + weight_decay * current
    )
    merged = merge_weight * inner + (1.0 - merge_weight) * new_global
    return (
        merged.astype(jnp.bfloat16)[None],
        first_new.astype(jnp.bfloat16)[None],
        second_new.astype(jnp.bfloat16)[None],
        new_global,
        new_momentum,
    )


def solution(mesh):
    placed = (
        P("island", "fsdp", None),
        P("island", "fsdp", None),
        P("island", "fsdp", None),
        P("fsdp", None),
        P("fsdp", None),
        P("island", "fsdp", None),
        P("island", "fsdp", None),
    )
    return jax.shard_map(
        local,
        mesh=mesh,
        in_specs=placed,
        out_specs=(
            P("island", "fsdp", None),
            P("island", "fsdp", None),
            P("island", "fsdp", None),
            P("fsdp", None),
            P("fsdp", None),
        ),
        check_vma=False,
    )
```

profile of v0, /device:TPU:0, one launch (start us, length us, event | category | flops | bytes accessed | tf_op | source)
XLA Modules:
  0.0 43.7 jit_solution(16846321739054371111)
XLA Ops:
  0.6 0.0 copy-start
  0.6 0.0 copy-start.1
  0.7 37.5 %shard_map.110 = (f32[1024,512]{1,0:T(8,128)S(1)}, bf16[1024,512]{1,0:T(8,128)(2,1)S(1)}) custom-call(bf16[1024,512]{1,0:T(8,128)(2,1)} %bitcast.30, bf16[128,4096]{1,0:T(8,128)(2,1)} %bitcast.31, bf16[128,512]{1,0:T(8,128)(2,1)} %bitcast.32), custom_call_target="tpu_custom_call" | custom-call | tf_op jit(solution)/shard_map/pallas_call | solution.py:298
  38.1 0.0 copy-done
  38.1 0.0 copy-done.1
  38.1 5.5 %fusion.10 = (bf16[1,1024,512]{2,1,0:T(8,128)(2,1)}, f32[1024,512]{1,0:T(8,128)}, f32[1024,512]{1,0:T(8,128)}, bf16[1,1024,512]{2,1,0:T(8,128)(2,1)}, bf16[1,1024,512]{2,1,0:T(8,128)(2,1)}) fusion(f32[1024,512]{1,0:T(8,128)S(1)} %get-tuple-element.7, bf16[1,1024,512]{2,1,0:T(8,128)(2,1)S(1)} %copy-done.1, bf16[1,1024,512]{2,1,0:T(8,128)(2,1)} %param.8, ...), kind=kLoop, calls=%fused_computation.17 | loop fusion | flops 15204352 | bytes 17825792 | tf_op jit(solution)/shard_map/broadcast_in_dim | solution.py:326
Async XLA Ops:
  0.6 37.5 %copy-start = (bf16[1,1024,512]{2,1,0:T(8,128)(2,1)S(1)}, bf16[1,1024,512]{2,1,0:T(8,128)(2,1)}, u32[]{:S(2)}) copy-start(bf16[1,1024,512]{2,1,0:T(8,128)(2,1)} %param.7) | copy-start | bytes 3145732
  0.6 37.5 %copy-start.1 = (bf16[1,1024,512]{2,1,0:T(8,128)(2,1)S(1)}, bf16[1,1024,512]{2,1,0:T(8,128)(2,1)}, u32[]{:S(2)}) copy-start(bf16[1,1024,512]{2,1,0:T(8,128)(2,1)} %param.9) | copy-start | bytes 3145732
where the time goes:
time: 43.8 us; the launch traced here: 43.7 us
  Pallas kernels  37.5 us (86%)
  other arithmetic  5.53 us (13%)
  between operations  0.67 us (2%)
    pallas_call x1, Pallas kernels, local(): pl.pallas_call(functools.partial(exchange, islands, shards, chunks, scale...  37.5 us
    broadcast_in_dim x1, other arithmetic, local(): merged.astype(jnp.bfloat16)[None]  5.53 us

commit v1 on v0

--- a/solution.py
+++ b/solution.py
@@ -250,6 +250,484 @@
         copy.wait_send()
 
 
+def token_splits(count):
+    if count % 64 == 0:
+        return (count // 2, count // 4, count // 4)
+    return (count,)
+
+
+def pieces_of(rows, islands, shards):
+    if shards != 4 or islands != 2 * shards:
+        return 0
+    for pieces in (8, 4, 2, 1):
+        if rows % (2 * pieces * 16) == 0:
+            return pieces
+    return 0
+
+
+def window(islands, pieces, splits, scale, *refs):
+    w_hbm, m_hbm, s_hbm, gw_hbm, om_hbm, x_hbm, cot_hbm = refs[:7]
+    nl, nf, ns, ng, nm = refs[7:12]
+    (wc, xc, xin, cot, own, psend, precv, kg, kgin, grad, half_inner, m, s, gw, om, mean,
+     rsin, pin, qin, pout, res,
+     lsem, lxsem, lcsem, rssem, keepsem, xosem, wsem, cosem, yxsem, xfsem, ypsem, yksem, fksem,
+     fisem, zpsem, zqsem, zrsem, agsem, dlsem) = refs[12:]
+    rows, width = mean.shape
+    half = rows // 2
+    size = half // pieces
+    count = 2 * pieces
+    f32, bf16 = jnp.float32, jnp.bfloat16
+
+    island = lax.axis_index("island")
+    shard = lax.axis_index("fsdp")
+    core = lax.rem(shard, 2)
+    chip = shard // 2
+    side = lax.rem(island, 2)
+    level = island // 2
+    inside = level * (3 - level) // 2
+
+    partner = (island, chip * 2 + 1 - core)
+
+    def across(c):
+        return (island, (1 - chip) * 2 + c)
+
+    def beside(c):
+        return (island + 1 - 2 * side, chip * 2 + c)
+
+    pair = ((level + 1 - 2 * lax.rem(level, 2)) * 2 + side, shard)
+    middle = ((3 - level) * 2 + side, shard)
+
+    offsets = [sum(splits[:i]) for i in range(len(splits))]
+
+    def block(c, i):
+        return pl.ds(2 * offsets[i] + c * splits[i], splits[i])
+
+    def both(i):
+        return pl.ds(2 * offsets[i], 2 * splits[i])
+
+    def source(i):
+        return pl.ds(offsets[i], splits[i])
+
+    def lanes(start, extent):
+        return pl.ds(pl.multiple_of(start, rows), extent)
+
+    my_lanes = lanes(chip * 2 * rows, 2 * rows)
+    core_rows = core * rows
+
+    barrier = pltpu.get_barrier_semaphore()
+
+    def greet(target):
+        pl.semaphore_signal(barrier, inc=1, device_id=target, device_id_type=MESH)
+
+    greet(partner)
+    greet(beside(1))
+    greet(across(0))
+
+    @pl.when(core == 0)
+    def _():
+        greet(across(1))
+
+    @pl.when(core == 1)
+    def _():
+        greet(beside(0))
+        greet(pair)
+
+    @pl.when((core == 1) & (inside == 1))
+    def _():
+        greet(middle)
+
+    tokens = []
+    wload = pltpu.make_async_copy(
+        w_hbm, wc.at[pl.ds(pl.multiple_of(core_rows, rows), rows)], lsem.at[0])
+    wload.start()
+    for i in range(len(splits)):
+        place = pl.ds(pl.multiple_of(2 * offsets[i] + core * splits[i], splits[i]), splits[i])
+        tokens.append(pltpu.make_async_copy(
+            x_hbm.at[source(i), my_lanes], xc.at[place], lxsem.at[i]))
+        tokens.append(pltpu.make_async_copy(cot_hbm.at[source(i)], cot.at[place], lcsem.at[i]))
+    for load in tokens:
+        load.start()
+
+    pl.semaphore_wait(barrier, 4 + core * (1 + inside))
+
+    def remote(src, dst, sems, index, target):
+        return pltpu.make_async_remote_copy(
+            src_ref=src, dst_ref=dst, send_sem=sems.at[0, index], recv_sem=sems.at[1, index],
+            device_id=target, device_id_type=MESH)
+
+    def token_send(c, i):
+        return remote(
+            x_hbm.at[source(i), lanes((1 - chip) * 2 * rows, 2 * rows)],
+            xin.at[block(c, i)], yxsem, 2 * i + c, across(0))
+
+    def kept(j):
+        return pl.multiple_of(side * half + j * size, size)
+
+    def given(j):
+        return pl.multiple_of((1 - side) * half + j * size, size)
+
+    def scatter_send(c, j):
+        return remote(
+            w_hbm.at[pl.ds(given(j), size)], rsin.at[2 * j + c], rssem, 2 * j + c, beside(1))
+
+    keep_send = remote(
+        w_hbm.at[pl.ds(pl.multiple_of(side * half, half), half)],
+        wc.at[pl.ds(pl.multiple_of(side * half, half), half)], keepsem, 0, partner)
+    weight_send = remote(w_hbm, wc.at[pl.ds(rows, rows)], wsem, 0, partner)
+
+    def own_tokens_up(i):
+        return remote(
+            x_hbm.at[source(i), lanes((chip * 2 + 1) * rows, rows)],
+            xc.at[block(0, i), pl.ds(rows, rows)], xosem, i, partner)
+
+    def own_tokens_down(i):
+        return remote(x_hbm.at[source(i), my_lanes], xc.at[block(1, i)], xosem, i, partner)
+
+    def cotangent_down(i):
+        return remote(cot_hbm.at[source(i)], cot.at[block(1, i)], cosem, i, partner)
+
+    def tokens_forward(i):
+        place = xin.at[both(i), pl.ds(rows, rows)]
+        return remote(place, place, xfsem, i, partner)
+
+    def partial_send(i):
+        return remote(psend.at[both(i)], precv.at[both(i)], ypsem, i, across(0))
+
+    def upstream_across(i):
+        return remote(kg.at[both(i)], kgin.at[both(i)], yksem, i, across(0))
+
+    def upstream_down(i):
+        return remote(kg.at[both(i)], kg.at[both(i)], fksem, i, partner)
+
+    def upstream_forward(i):
+        return remote(kgin.at[both(i)], kgin.at[both(i)], fisem, i, partner)
+
+    def outer_send(k):
+        return remote(pout.at[k], pin.at[k], zpsem, k, pair)
+
+    def middle_send(k):
+        return remote(pout.at[k], qin.at[k], zqsem, k, middle)
+
+    def result_send(k):
+        return remote(res.at[k], res.at[k], zrsem, k, pair)
+
+    def gather_send(k):
+        return remote(
+            res.at[k], mean.at[pl.ds(kept(k // 2), size)], agsem, k, beside(k % 2))
+
+    def deliver_send(j):
+        return remote(res.at[2 * j], mean.at[pl.ds(kept(j), size)], dlsem, j, partner)
+
+    def gather_recv(k):
+        return remote(
+            res.at[k], mean.at[pl.ds(given(k // 2), size)], agsem, k, beside(k % 2))
+
+    state_loads = [
+        pltpu.make_async_copy(place, dst, lsem.at[1 + index])
+        for index, (place, dst) in enumerate(((m_hbm, m), (s_hbm, s), (gw_hbm, gw), (om_hbm, om)))
+    ]
+
+    def own_gradient(base):
+        tile = min(256, rows)
+
+        @pl.loop(0, rows // tile)
+        def _(t):
+            start = pl.multiple_of(t * tile, tile)
+            grad[pl.ds(start, tile), :] = lax.dot_general(
+                xc[:, pl.ds(pl.multiple_of(base + start, tile), tile)], kg[...],
+                (((0,), (0,)), ((), ())), preferred_element_type=f32)
+
+    def gradient_tile(base, start, tile):
+        grad[pl.ds(start, tile), :] += lax.dot_general(
+            xin[:, pl.ds(pl.multiple_of(base + start, tile), tile)], kgin[...],
+            (((0,), (0,)), ((), ())), preferred_element_type=f32)
+        step = min(32, tile)
+
+        @pl.loop(0, tile // step)
+        def _(u):
+            place = pl.ds(pl.multiple_of(start + u * step, step), step)
+            gradient = grad[place, :]
+            first_new = beta_one * m[place, :].astype(f32) + (1.0 - beta_one) * gradient
+            second_new = (
+                beta_two * s[place, :].astype(f32) + (1.0 - beta_two) * gradient * gradient)
+            nf[place, :] = first_new.astype(bf16)
+            ns[place, :] = second_new.astype(bf16)
+            current = wc[pl.ds(pl.multiple_of(base + start + u * step, step), step), :].astype(f32)
+            inner = current - inner_rate * (
+                first_new / (jnp.sqrt(second_new) + adam_epsilon) + weight_decay * current)
+            half_inner[place, :] = merge_weight * inner
+
+    def inner_update(base):
+        tile = min(256, rows)
+
+        @pl.loop(0, rows // tile)
+        def _(t):
+            gradient_tile(base, pl.multiple_of(t * tile, tile), tile)
+
+    def outer_update(start, extent):
+        step = min(32, extent)
+
+        @pl.loop(0, extent // step)
+        def _(u):
+            place = pl.ds(pl.multiple_of(start + u * step, step), step)
+            weights = gw[place, :]
+            outer_grad = weights - mean[place, :].astype(f32)
+            momentum = outer_beta * om[place, :] + outer_grad
+            updated = weights - outer_rate * (outer_grad + outer_beta * momentum)
+            nm[place, :] = momentum
+            ng[place, :] = updated
+            nl[place, :] = (half_inner[place, :] + (1.0 - merge_weight) * updated).astype(bf16)
+
+    def matmul(out, place, left, convert):
+        part = min(256, width)
+
+        @pl.loop(0, width // part)
+        def _(n):
+            columns = pl.ds(pl.multiple_of(n * part, part), part)
+            value = jnp.dot(left[...], wc[:, columns], preferred_element_type=f32)
+            out[place, columns] = value.astype(bf16) if convert else value
+
+    steps = range(len(splits))
+
+    @pl.when(core == 0)
+    def _():
+        sends = []
+
+        def begin(copy):
+            copy.start()
+            sends.append(copy)
+
+        begin(token_send(0, 0))
+        begin(scatter_send(0, 0))
+        begin(keep_send)
+        for j in range(1, pieces):
+            begin(scatter_send(0, j))
+        for i in steps[1:]:
+            begin(token_send(0, i))
+        for i in steps:
+            begin(own_tokens_up(i))
+        for load in state_loads:
+            load.start()
+        wload.wait()
+        for load in tokens:
+            load.wait()
+        weight_send.wait_recv()
+        for i in steps:
+            own_tokens_down(i).wait_recv()
+        matmul(own, slice(None), xc, False)
+        for i in steps:
+            token_send(0, i).wait_recv()
+            token_send(1, i).wait_recv()
+            begin(tokens_forward(i))
+            matmul(psend, both(i), xin.at[both(i)], True)
+            begin(partial_send(i))
+        for i in steps:
+            cotangent_down(i).wait_recv()
+        for i in steps:
+            partial_send(i).wait_recv()
+            for head in range(width // HEAD_DIM):
+                columns = slice(head * HEAD_DIM, (head + 1) * HEAD_DIM)
+                keys = (own[both(i), columns] + precv[both(i), columns].astype(f32)) * scale
+                kg[both(i), columns] = head_backward(
+                    keys, cot[both(i), columns].astype(f32), scale)
+            begin(upstream_across(i))
+            begin(upstream_down(i))
+        own_gradient(0)
+        for i in steps:
+            upstream_across(i).wait_recv()
+            begin(upstream_forward(i))
+        for load in state_loads:
+            load.wait()
+        inner_update(0)
+        for j in range(pieces):
+            deliver_send(j).wait_recv()
+            outer_update(kept(j), size)
+            gather_recv(2 * j).wait_recv()
+            outer_update(given(j), size)
+        for copy in sends:
+            copy.wait_send()
+
+    @pl.when(core == 1)
+    def _():
+        sends = []
+
+        def begin(copy):
+            copy.start()
+            sends.append(copy)
+
+        def held(k):
+            place = pl.ds(pl.multiple_of((k % 2) * rows + kept(k // 2), size), size)
+            return wc[place, :].astype(f32) + rsin[k].astype(f32)
+
+        def hand_out(k):
+            gather_send(k).start()
+            if k % 2:
+                mean[pl.ds(kept(k // 2), size), :] = res[k]
+            else:
+                deliver_send(k // 2).start()
+
+        begin(token_send(1, 0))
+        for j in range(pieces):
+            begin(scatter_send(1, j))
+        for i in steps[1:]:
+            begin(token_send(1, i))
+        begin(weight_send)
+        for i in steps:
+            begin(own_tokens_down(i))
+            begin(cotangent_down(i))
+        for load in state_loads:
+            load.start()
+        wload.wait()
+        for load in tokens:
+            load.wait()
+        keep_send.wait_recv()
+
+        @pl.when(inside == 0)
+        def _():
+            for k in range(count):
+                scatter_send(k % 2, k // 2).wait_recv()
+                pout[k] = held(k).astype(bf16)
+                outer_send(k).start()
+            for k in range(count):
+                result_send(k).wait_recv()
+                hand_out(k)
+            for k in range(count):
+                outer_send(k).wait_send()
+
+        @pl.when(inside == 1)
+        def _():
+            lag = min(4, count)
+            for k in range(count + lag):
+                if k < count:
+                    scatter_send(k % 2, k // 2).wait_recv()
+                    outer_send(k).wait_recv()
+                    pout[k] = (held(k) + pin[k].astype(f32)).astype(bf16)
+                    middle_send(k).start()
+                if k >= lag:
+                    q = k - lag
+                    middle_send(q).wait_recv()
+                    total = pout[q].astype(f32) + qin[q].astype(f32)
+                    res[q] = (total / islands).astype(bf16)
+                    result_send(q).start()
+                    hand_out(q)
+            for k in range(count):
+                middle_send(k).wait_send()
+                result_send(k).wait_send()
+
+        for i in steps:
+            own_tokens_up(i).wait_recv()
+            upstream_down(i).wait_recv()
+        own_gradient(rows)
+        for i in steps:
+            tokens_forward(i).wait_recv()
+            upstream_forward(i).wait_recv()
+        for load in state_loads:
+            load.wait()
+        inner_update(rows)
+        for j in range(pieces):
+            outer_update(kept(j), size)
+        for j in range(pieces):
+            gather_recv(2 * j + 1).wait_recv()
+            outer_update(given(j), size)
+        for k in range(count):
+            gather_send(k).wait_send()
+        for j in range(pieces):
+            deliver_send(j).wait_send()
+        for copy in sends:
+            copy.wait_send()
+
+
+def write_back(*refs):
+    arrays = len(refs) // 2
+    sems = refs[-1]
+    copies = []
+    for index in range(arrays):
+        part = refs[index].shape[0] // 2
+        for piece in range(2):
+            place = pl.ds(piece * part, part)
+            copies.append(pltpu.make_async_copy(
+                refs[index].at[place], refs[arrays + index].at[place], sems.at[index, piece]))
+    for copy in copies:
+        copy.start()
+    for copy in copies:
+        copy.wait()
+
+
+def fused(pieces, local_weights, adam_first, adam_second, global_weights, outer_momentum, inputs,
+          key_cotangent):
+    arrays = (local_weights[0], adam_first[0], adam_second[0], global_weights, outer_momentum,
+              inputs[0], key_cotangent[0])
+    rows, width = arrays[0].shape
+    count, depth = arrays[5].shape
+    islands = lax.axis_size("island")
+    splits = token_splits(count)
+    size = rows // (2 * pieces)
+    bf16, f32 = jnp.bfloat16, jnp.float32
+    dma, vmem = pltpu.SemaphoreType.DMA, pltpu.VMEM
+    out_shape = [jax.ShapeDtypeStruct((rows, width), bf16)] * 3 + [
+        jax.ShapeDtypeStruct((rows, width), f32)] * 2
+    steps = len(splits)
+    scratch = [
+        vmem((2 * rows, width), bf16),
+        vmem((2 * count, 2 * rows), bf16),
+        vmem((2 * count, 2 * rows), bf16),
+        vmem((2 * count, width), bf16),
+        vmem((2 * count, width), f32),
+        vmem((2 * count, width), bf16),
+        vmem((2 * count, width), bf16),
+        vmem((2 * count, width), bf16),
+        vmem((2 * count, width), bf16),
+        vmem((rows, width), f32),
+        vmem((rows, width), f32),
+        vmem((rows, width), bf16),
+        vmem((rows, width), bf16),
+        vmem((rows, width), f32),
+        vmem((rows, width), f32),
+        vmem((rows, width), bf16),
+    ] + [vmem((2 * pieces, size, width), bf16)] * 5 + [
+        dma((5,)),
+        dma((steps,)),
+        dma((steps,)),
+        dma((2, 2 * pieces)),
+        dma((2, 1)),
+        dma((2, steps)),
+        dma((2, 1)),
+        dma((2, steps)),
+        dma((2, 2 * steps)),
+        dma((2, steps)),
+        dma((2, steps)),
+        dma((2, steps)),
+        dma((2, steps)),
+        dma((2, steps)),
+        dma((2, 2 * pieces)),
+        dma((2, 2 * pieces)),
+        dma((2, 2 * pieces)),
+        dma((2, 2 * pieces)),
+        dma((2, pieces)),
+    ]
+    in_vmem = pl.BlockSpec(memory_space=pltpu.VMEM)
+    in_hbm = pl.BlockSpec(memory_space=pltpu.HBM)
+    results = pl.pallas_call(
+        functools.partial(window, islands, pieces, splits, float(depth) ** (-0.5)),
+        out_shape=out_shape,
+        in_specs=[in_hbm] * len(arrays),
+        out_specs=[in_vmem] * len(out_shape),
+        scratch_shapes=scratch,
+        compiler_params=pltpu.CompilerParams(
+            collective_id=0, has_side_effects=True, vmem_limit_bytes=40 * 1024 * 1024
+        ),
+    )(*(pltpu.with_memory_space_constraint(a, pltpu.HBM) for a in arrays))
+    written = pl.pallas_call(
+        write_back,
+        out_shape=out_shape,
+        in_specs=[in_vmem] * len(out_shape),
+        out_specs=[in_hbm] * len(out_shape),
+        scratch_shapes=[dma((len(out_shape), 2))],
+        compiler_params=pltpu.CompilerParams(vmem_limit_bytes=4 * 1024 * 1024),
+    )(*results)
+    return tuple(a[None] for a in written[:3]) + tuple(written[3:])
+
+
 def local(
     local_weights, adam_first, adam_second, global_weights, outer_momentum, inputs, key_cotangent
 ):
@@ -261,6 +739,10 @@
     islands, shards = lax.axis_size("island"), lax.axis_size("fsdp")
     chips = shards // 2
     others = max(chips - 1, 1)
+    pieces = pieces_of(rows, islands, shards)
+    if pieces and width % HEAD_DIM == 0:
+        return fused(pieces, local_weights, adam_first, adam_second, global_weights,
+                     outer_momentum, inputs, key_cotangent)
     chunks = chunk_count(rows, islands)
     bf16, f32 = jnp.bfloat16, jnp.float32
     dma = pltpu.SemaphoreType.DMA

time: 43.8 us -> 38.8 us (0.89)
  the two profiles are of different devices: /device:TPU:0 before, /device:TPU:1 now
where the time goes in v1:
time: 38.8 us; the launch traced here: 38.7 us
  Pallas kernels  38 us (98%)
  between operations  0.64 us (2%)
    pallas_call x1, Pallas kernels, fused(): pl.pallas_call(functools.partial(window, islands, pieces, splits, float(d...  35 us
    pallas_call x1, Pallas kernels, fused(): pl.pallas_call(write_back, out_shape=out_shape, in_specs=[in_vmem] * len(...  3.07 us

profile of v1, /device:TPU:1, one launch (start us, length us, event | category | flops | bytes accessed | tf_op | source)
XLA Modules:
  0.0 38.7 jit_solution(15567276308226205486)
XLA Ops:
  0.6 35.0 %shard_map.110 = (bf16[1024,512]{1,0:T(8,128)(2,1)S(1)}, bf16[1024,512]{1,0:T(8,128)(2,1)S(1)}, bf16[1024,512]{1,0:T(8,128)(2,1)S(1)}, f32[1024,512]{1,0:T(8,128)S(1)}, f32[1024,512]{1,0:T(8,128)S(1)}) custom-call(bf16[1024,512]{1,0:T(8,128)(2,1)} %bitcast.8, bf16[1024,512]{1,0:T(8,128)(2,1)} %bitcast.9, bf16[1024,512]{1,0:T(8,128)(2,1)} %bitcast.10, ...), custom_call_target="tpu_custom_call" | custom-call | tf_op jit(solution)/shard_map/pallas_call | solution.py:710
  35.6 3.1 %shard_map.111 = (bf16[1024,512]{1,0:T(8,128)(2,1)}, bf16[1024,512]{1,0:T(8,128)(2,1)}, bf16[1024,512]{1,0:T(8,128)(2,1)}, f32[1024,512]{1,0:T(8,128)}, f32[1024,512]{1,0:T(8,128)}) custom-call(bf16[1024,512]{1,0:T(8,128)(2,1)S(1)} %get-tuple-element.15.refs_0_, bf16[1024,512]{1,0:T(8,128)(2,1)S(1)} %get-tuple-element.16.refs_1_, ...), custom_call_target="tpu_custom_call" | custom-call | tf_op jit(solution)/shard_map/pallas_call | solution.py:720

commit v2 on v1

--- a/solution.py
+++ b/solution.py
@@ -258,11 +258,12 @@
 
 def pieces_of(rows, islands, shards):
     if shards != 4 or islands != 2 * shards:
-        return 0
-    for pieces in (8, 4, 2, 1):
-        if rows % (2 * pieces * 16) == 0:
-            return pieces
-    return 0
+        return ()
+    for grades in ((1,) * 8, (1,) * 4, (1,)):
+        unit, rest = divmod(rows // 2, sum(grades))
+        if rest == 0 and unit % 16 == 0:
+            return tuple(unit * grade for grade in grades)
+    return ()
 
 
 def window(islands, pieces, splits, scale, *refs):
@@ -270,12 +271,13 @@
     nl, nf, ns, ng, nm = refs[7:12]
     (wc, xc, xin, cot, own, psend, precv, kg, kgin, grad, half_inner, m, s, gw, om, mean,
      rsin, pin, qin, pout, res,
-     lsem, lxsem, lcsem, rssem, keepsem, xosem, wsem, cosem, yxsem, xfsem, ypsem, yksem, fksem,
-     fisem, zpsem, zqsem, zrsem, agsem, dlsem) = refs[12:]
+     load_sem, sent, first, rail, cross, gathered, kept_sem, passed) = refs[12:]
     rows, width = mean.shape
     half = rows // 2
-    size = half // pieces
-    count = 2 * pieces
+    groups = range(len(pieces))
+    token_count = x_hbm.shape[0]
+    count = 2 * len(pieces)
+    begins = [sum(pieces[:j]) for j in groups]
     f32, bf16 = jnp.float32, jnp.bfloat16
 
     island = lax.axis_index("island")
@@ -338,92 +340,152 @@
 
     tokens = []
     wload = pltpu.make_async_copy(
-        w_hbm, wc.at[pl.ds(pl.multiple_of(core_rows, rows), rows)], lsem.at[0])
+        w_hbm, wc.at[pl.ds(pl.multiple_of(core_rows, rows), rows)], load_sem.at[0])
     wload.start()
     for i in range(len(splits)):
         place = pl.ds(pl.multiple_of(2 * offsets[i] + core * splits[i], splits[i]), splits[i])
         tokens.append(pltpu.make_async_copy(
-            x_hbm.at[source(i), my_lanes], xc.at[place], lxsem.at[i]))
-        tokens.append(pltpu.make_async_copy(cot_hbm.at[source(i)], cot.at[place], lcsem.at[i]))
+            x_hbm.at[source(i), my_lanes], xc.at[place], load_sem.at[1]))
+        tokens.append(pltpu.make_async_copy(
+            cot_hbm.at[source(i)], cot.at[place], load_sem.at[2]))
     for load in tokens:
         load.start()
 
     pl.semaphore_wait(barrier, 4 + core * (1 + inside))
 
-    def remote(src, dst, sems, index, target):
+    def remote(src, dst, kind, into, target):
         return pltpu.make_async_remote_copy(
-            src_ref=src, dst_ref=dst, send_sem=sems.at[0, index], recv_sem=sems.at[1, index],
+            src_ref=src, dst_ref=dst, send_sem=sent.at[kind], recv_sem=into,
             device_id=target, device_id_type=MESH)
+
+    def all_tokens(ref):
+        return ref.at[pl.ds(0, token_count)]
+
+    def tokens_loaded():
+        for ref, dst, index in ((x_hbm.at[:, my_lanes], xc, 1), (cot_hbm, cot, 2)):
+            pltpu.make_async_copy(ref, all_tokens(dst), load_sem.at[index]).wait()
+
+    def kept(j):
+        return pl.multiple_of(side * half + begins[j], 16)
+
+    def given(j):
+        return pl.multiple_of((1 - side) * half + begins[j], 16)
+
+    def kept_rows(j):
+        return pl.ds(kept(j), pieces[j])
+
+    def given_rows(j):
+        return pl.ds(given(j), pieces[j])
+
+    def slot(k):
+        return pl.ds(2 * begins[k // 2] + (k % 2) * pieces[k // 2], pieces[k // 2])
+
+    group = len(pieces)
+    parts = len(splits)
+
+    def scatter_send(c, j):
+        k = 2 * j + c
+        return remote(w_hbm.at[given_rows(j)], rsin.at[slot(k)], 0, first.at[k], beside(1))
+
+    def scatter_total():
+        return remote(
+            w_hbm.at[pl.ds(0, half)], rsin.at[pl.ds(0, half)], 0, first.at[0], beside(1))
 
     def token_send(c, i):
         return remote(
             x_hbm.at[source(i), lanes((1 - chip) * 2 * rows, 2 * rows)],
-            xin.at[block(c, i)], yxsem, 2 * i + c, across(0))
-
-    def kept(j):
-        return pl.multiple_of(side * half + j * size, size)
-
-    def given(j):
-        return pl.multiple_of((1 - side) * half + j * size, size)
-
-    def scatter_send(c, j):
+            xin.at[block(c, i)], 1, first.at[group + 2 * i + c], across(0))
+
+    def token_total():
         return remote(
-            w_hbm.at[pl.ds(given(j), size)], rsin.at[2 * j + c], rssem, 2 * j + c, beside(1))
-
-    keep_send = remote(
-        w_hbm.at[pl.ds(pl.multiple_of(side * half, half), half)],
-        wc.at[pl.ds(pl.multiple_of(side * half, half), half)], keepsem, 0, partner)
-    weight_send = remote(w_hbm, wc.at[pl.ds(rows, rows)], wsem, 0, partner)
+            x_hbm.at[:, lanes((1 - chip) * 2 * rows, 2 * rows)],
+            all_tokens(xin), 1, first.at[group], across(0))
+
+    def keep_send(j):
+        extent = pieces[j] if j < 2 else half - begins[j]
+        place = pl.ds(kept(j), extent)
+        return remote(w_hbm.at[place], wc.at[place], 2, kept_sem.at[j], partner)
+
+    def keep_total():
+        return remote(
+            w_hbm.at[pl.ds(0, half)], wc.at[pl.ds(0, half)], 2, kept_sem.at[0], partner)
+
+    weight_send = remote(w_hbm, wc.at[pl.ds(rows, rows)], 2, cross.at[0], partner)
 
     def own_tokens_up(i):
         return remote(
             x_hbm.at[source(i), lanes((chip * 2 + 1) * rows, rows)],
-            xc.at[block(0, i), pl.ds(rows, rows)], xosem, i, partner)
+            xc.at[block(0, i), pl.ds(rows, rows)], 3, passed.at[0], partner)
+
+    def own_tokens_up_total():
+        return remote(
+            x_hbm.at[:, lanes((chip * 2 + 1) * rows, rows)],
+            xc.at[pl.ds(0, token_count), pl.ds(rows, rows)], 3, passed.at[0], partner)
 
     def own_tokens_down(i):
-        return remote(x_hbm.at[source(i), my_lanes], xc.at[block(1, i)], xosem, i, partner)
+        return remote(
+            x_hbm.at[source(i), my_lanes], xc.at[block(1, i)], 3, passed.at[0], partner)
+
+    def own_tokens_down_total():
+        return remote(x_hbm.at[:, my_lanes], all_tokens(xc), 3, passed.at[0], partner)
 
     def cotangent_down(i):
-        return remote(cot_hbm.at[source(i)], cot.at[block(1, i)], cosem, i, partner)
-
-    def tokens_forward(i):
-        place = xin.at[both(i), pl.ds(rows, rows)]
-        return remote(place, place, xfsem, i, partner)
-
-    def partial_send(i):
-        return remote(psend.at[both(i)], precv.at[both(i)], ypsem, i, across(0))
-
-    def upstream_across(i):
-        return remote(kg.at[both(i)], kgin.at[both(i)], yksem, i, across(0))
-
-    def upstream_down(i):
-        return remote(kg.at[both(i)], kg.at[both(i)], fksem, i, partner)
-
-    def upstream_forward(i):
-        return remote(kgin.at[both(i)], kgin.at[both(i)], fisem, i, partner)
-
-    def outer_send(k):
-        return remote(pout.at[k], pin.at[k], zpsem, k, pair)
-
-    def middle_send(k):
-        return remote(pout.at[k], qin.at[k], zqsem, k, middle)
-
-    def result_send(k):
-        return remote(res.at[k], res.at[k], zrsem, k, pair)
+        return remote(cot_hbm.at[source(i)], cot.at[block(1, i)], 4, passed.at[1], partner)
+
+    def cotangent_total():
+        return remote(cot_hbm, all_tokens(cot), 4, passed.at[1], partner)
+
+    def tokens_forward(place):
+        part = xin.at[place, pl.ds(rows, rows)]
+        return remote(part, part, 4, passed.at[1], partner)
+
+    def partial_send(place, i):
+        return remote(psend.at[place], precv.at[place], 5, rail.at[i], across(0))
+
+    def upstream_across(place, i):
+        return remote(kg.at[place], kgin.at[place], 6, rail.at[parts + i], across(0))
+
+    def upstream_down(place):
+        return remote(kg.at[place], kg.at[place], 7, passed.at[2], partner)
+
+    def upstream_forward(place):
+        return remote(kgin.at[place], kgin.at[place], 8, passed.at[3], partner)
 
     def gather_send(k):
         return remote(
-            res.at[k], mean.at[pl.ds(kept(k // 2), size)], agsem, k, beside(k % 2))
+            res.at[slot(k)], mean.at[kept_rows(k // 2)], 5, gathered.at[k // 2], beside(k % 2))
+
+    def gather_total():
+        return remote(res, mean, 5, gathered.at[0], beside(0))
+
+    def gather_recv(j):
+        return remote(
+            res.at[slot(2 * j)], mean.at[given_rows(j)], 5, gathered.at[j], beside(0))
 
     def deliver_send(j):
-        return remote(res.at[2 * j], mean.at[pl.ds(kept(j), size)], dlsem, j, partner)
-
-    def gather_recv(k):
+        return remote(res.at[slot(2 * j)], mean.at[kept_rows(j)], 6, first.at[j], partner)
+
+    def deliver_total():
         return remote(
-            res.at[k], mean.at[pl.ds(given(k // 2), size)], agsem, k, beside(k % 2))
+            res.at[pl.ds(0, half)], mean.at[pl.ds(0, half)], 6, first.at[0], partner)
+
+    def outer_send(k):
+        return remote(pout.at[slot(k)], pin.at[slot(k)], 7, rail.at[k], pair)
+
+    def middle_send(k):
+        return remote(pout.at[slot(k)], qin.at[slot(k)], 7, cross.at[k], middle)
+
+    def part_total():
+        return remote(pout, pin, 7, rail.at[0], pair)
+
+    def result_send(k):
+        return remote(res.at[slot(k)], res.at[slot(k)], 8, rail.at[k], pair)
+
+    def result_total():
+        return remote(res, res, 8, rail.at[0], pair)
 
     state_loads = [
-        pltpu.make_async_copy(place, dst, lsem.at[1 + index])
+        pltpu.make_async_copy(place, dst, load_sem.at[3 + index])
         for index, (place, dst) in enumerate(((m_hbm, m), (s_hbm, s), (gw_hbm, gw), (om_hbm, om)))
     ]
 
@@ -465,7 +527,7 @@
             gradient_tile(base, pl.multiple_of(t * tile, tile), tile)
 
     def outer_update(start, extent):
-        step = min(32, extent)
+        step = 32 if extent % 32 == 0 else 16
 
         @pl.loop(0, extent // step)
         def _(u):
@@ -476,7 +538,15 @@
             updated = weights - outer_rate * (outer_grad + outer_beta * momentum)
             nm[place, :] = momentum
             ng[place, :] = updated
-            nl[place, :] = (half_inner[place, :] + (1.0 - merge_weight) * updated).astype(bf16)
+
+    def merge(start, extent):
+        step = 32 if extent % 32 == 0 else 16
+
+        @pl.loop(0, extent // step)
+        def _(u):
+            place = pl.ds(pl.multiple_of(start + u * step, step), step)
+            nl[place, :] = (
+                half_inner[place, :] + (1.0 - merge_weight) * ng[place, :]).astype(bf16)
 
     def matmul(out, place, left, convert):
         part = min(256, width)
@@ -489,152 +559,173 @@
 
     steps = range(len(splits))
 
+    every = slice(None)
+
     @pl.when(core == 0)
     def _():
-        sends = []
-
-        def begin(copy):
-            copy.start()
-            sends.append(copy)
-
-        begin(token_send(0, 0))
-        begin(scatter_send(0, 0))
-        begin(keep_send)
-        for j in range(1, pieces):
-            begin(scatter_send(0, j))
-        for i in steps[1:]:
-            begin(token_send(0, i))
+        for j in groups:
+            scatter_send(0, j).start()
+            if j < 3:
+                keep_send(j).start()
+            if j < 2 and j < parts:
+                token_send(0, j).start()
         for i in steps:
-            begin(own_tokens_up(i))
+            own_tokens_up(i).start()
         for load in state_loads:
             load.start()
         wload.wait()
-        for load in tokens:
-            load.wait()
+        tokens_loaded()
         weight_send.wait_recv()
-        for i in steps:
-            own_tokens_down(i).wait_recv()
-        matmul(own, slice(None), xc, False)
+        own_tokens_down_total().wait_recv()
+        matmul(own, every, xc, False)
         for i in steps:
             token_send(0, i).wait_recv()
             token_send(1, i).wait_recv()
-            begin(tokens_forward(i))
+            tokens_forward(both(i)).start()
             matmul(psend, both(i), xin.at[both(i)], True)
-            begin(partial_send(i))
+            partial_send(both(i), i).start()
+            if i == 0:
+                for later in steps[2:]:
+                    token_send(0, later).start()
+        cotangent_total().wait_recv()
         for i in steps:
-            cotangent_down(i).wait_recv()
-        for i in steps:
-            partial_send(i).wait_recv()
+            partial_send(both(i), i).wait_recv()
             for head in range(width // HEAD_DIM):
                 columns = slice(head * HEAD_DIM, (head + 1) * HEAD_DIM)
                 keys = (own[both(i), columns] + precv[both(i), columns].astype(f32)) * scale
                 kg[both(i), columns] = head_backward(
                     keys, cot[both(i), columns].astype(f32), scale)
-            begin(upstream_across(i))
-            begin(upstream_down(i))
+            upstream_across(both(i), i).start()
+            upstream_down(both(i)).start()
         own_gradient(0)
         for i in steps:
-            upstream_across(i).wait_recv()
-            begin(upstream_forward(i))
+            upstream_across(both(i), i).wait_recv()
+            upstream_forward(both(i)).start()
         for load in state_loads:
             load.wait()
         inner_update(0)
-        for j in range(pieces):
+        for j in groups:
             deliver_send(j).wait_recv()
-            outer_update(kept(j), size)
-            gather_recv(2 * j).wait_recv()
-            outer_update(given(j), size)
-        for copy in sends:
-            copy.wait_send()
+            outer_update(kept(j), pieces[j])
+            merge(kept(j), pieces[j])
+            gather_recv(j).wait_recv()
+            outer_update(given(j), pieces[j])
+            merge(given(j), pieces[j])
+        for total in (scatter_total(), token_total(), keep_total(), own_tokens_up_total(),
+                      tokens_forward(every), partial_send(every, 0), upstream_across(every, 0),
+                      upstream_down(every), upstream_forward(every)):
+            total.wait_send()
 
     @pl.when(core == 1)
     def _():
-        sends = []
-
-        def begin(copy):
-            copy.start()
-            sends.append(copy)
-
         def held(k):
-            place = pl.ds(pl.multiple_of((k % 2) * rows + kept(k // 2), size), size)
-            return wc[place, :].astype(f32) + rsin[k].astype(f32)
+            j = k // 2
+            place = pl.ds(pl.multiple_of((k % 2) * rows + kept(j), 16), pieces[j])
+            return wc[place, :].astype(f32) + rsin[slot(k), :].astype(f32)
 
         def hand_out(k):
             gather_send(k).start()
+            j = k // 2
             if k % 2:
-                mean[pl.ds(kept(k // 2), size), :] = res[k]
+                mean[kept_rows(j), :] = res[slot(k), :]
+                outer_update(kept(j), pieces[j])
             else:
-                deliver_send(k // 2).start()
-
-        begin(token_send(1, 0))
-        for j in range(pieces):
-            begin(scatter_send(1, j))
-        for i in steps[1:]:
-            begin(token_send(1, i))
-        begin(weight_send)
+                deliver_send(j).start()
+
+        for j in groups:
+            scatter_send(1, j).start()
+            if j < parts:
+                token_send(1, j).start()
+        weight_send.start()
         for i in steps:
-            begin(own_tokens_down(i))
-            begin(cotangent_down(i))
+            own_tokens_down(i).start()
+            cotangent_down(i).start()
         for load in state_loads:
             load.start()
         wload.wait()
-        for load in tokens:
-            load.wait()
-        keep_send.wait_recv()
+        state_loads[2].wait()
+        state_loads[3].wait()
+
+        def arrived(k):
+            scatter_send(k % 2, k // 2).wait_recv()
+            if k % 2 == 0 and k < 6:
+                keep_send(k // 2).wait_recv()
+
+        def outer_part(k):
+            arrived(k)
+            pout[slot(k), :] = held(k).astype(bf16)
+            outer_send(k).start()
+
+        def outer_result(k):
+            result_send(k).wait_recv()
+            hand_out(k)
+
+        def middle_part(k):
+            arrived(k)
+            outer_send(k).wait_recv()
+            pout[slot(k), :] = (held(k) + pin[slot(k), :].astype(f32)).astype(bf16)
+            middle_send(k).start()
+
+        def middle_result(k):
+            middle_send(k).wait_recv()
+            total = pout[slot(k), :].astype(f32) + qin[slot(k), :].astype(f32)
+            res[slot(k), :] = (total / islands).astype(bf16)
+            result_send(k).start()
+            hand_out(k)
+
+        tile = min(256, rows)
+        tiles = rows // tile
+
+        def gradient_start():
+            tokens_loaded()
+            own_tokens_up_total().wait_recv()
+            upstream_down(every).wait_recv()
+            own_gradient(rows)
+
+        def gradient_ready():
+            tokens_forward(every).wait_recv()
+            upstream_forward(every).wait_recv()
+            for load in state_loads[:2]:
+                load.wait()
+
+        def interleave(first, second, lag, own_at, tiles_at):
+            work = {}
+            work.setdefault(min(own_at, count - 1), []).append(gradient_start)
+            for t in range(tiles):
+                place = work.setdefault(min(tiles_at + t, count - 1), [])
+                if t == 0:
+                    place.append(gradient_ready)
+                place.append(functools.partial(gradient_tile, rows, t * tile, tile))
+            done = 0
+            for k in range(count + lag):
+                if k < count:
+                    first(k)
+                if k >= lag:
+                    second(k - lag)
+                    for item in work.get(k - lag, ()):
+                        item()
 
         @pl.when(inside == 0)
         def _():
-            for k in range(count):
-                scatter_send(k % 2, k // 2).wait_recv()
-                pout[k] = held(k).astype(bf16)
-                outer_send(k).start()
-            for k in range(count):
-                result_send(k).wait_recv()
-                hand_out(k)
-            for k in range(count):
-                outer_send(k).wait_send()
+            interleave(outer_part, outer_result, count, count * 10 // 16, count * 14 // 16)
 
         @pl.when(inside == 1)
         def _():
-            lag = min(4, count)
-            for k in range(count + lag):
-                if k < count:
-                    scatter_send(k % 2, k // 2).wait_recv()
-                    outer_send(k).wait_recv()
-                    pout[k] = (held(k) + pin[k].astype(f32)).astype(bf16)
-                    middle_send(k).start()
-                if k >= lag:
-                    q = k - lag
-                    middle_send(q).wait_recv()
-                    total = pout[q].astype(f32) + qin[q].astype(f32)
-                    res[q] = (total / islands).astype(bf16)
-                    result_send(q).start()
-                    hand_out(q)
-            for k in range(count):
-                middle_send(k).wait_send()
-                result_send(k).wait_send()
-
-        for i in steps:
-            own_tokens_up(i).wait_recv()
-            upstream_down(i).wait_recv()
-        own_gradient(rows)
-        for i in steps:
-            tokens_forward(i).wait_recv()
-            upstream_forward(i).wait_recv()
-        for load in state_loads:
-            load.wait()
-        inner_update(rows)
-        for j in range(pieces):
-            outer_update(kept(j), size)
-        for j in range(pieces):
-            gather_recv(2 * j + 1).wait_recv()
-            outer_update(given(j), size)
-        for k in range(count):
-            gather_send(k).wait_send()
-        for j in range(pieces):
-            deliver_send(j).wait_send()
-        for copy in sends:
-            copy.wait_send()
+            interleave(middle_part, middle_result, min(4, count), count, count)
+
+        merge(pl.multiple_of(side * half, half), half)
+        for j in groups:
+            gather_recv(j).wait_recv()
+            outer_update(given(j), pieces[j])
+            merge(given(j), pieces[j])
+
+        @pl.when(inside == 1)
+        def _():
+            result_total().wait_send()
+
+        for total in (scatter_total(), token_total(), weight_send, own_tokens_down_total(),
+                      cotangent_total(), gather_total(), deliver_total(), part_total()):
+            total.wait_send()
 
 
 def write_back(*refs):
@@ -661,7 +752,7 @@
     count, depth = arrays[5].shape
     islands = lax.axis_size("island")
     splits = token_splits(count)
-    size = rows // (2 * pieces)
+    groups = len(pieces)
     bf16, f32 = jnp.bfloat16, jnp.float32
     dma, vmem = pltpu.SemaphoreType.DMA, pltpu.VMEM
     out_shape = [jax.ShapeDtypeStruct((rows, width), bf16)] * 3 + [
@@ -684,26 +775,15 @@
         vmem((rows, width), f32),
         vmem((rows, width), f32),
         vmem((rows, width), bf16),
-    ] + [vmem((2 * pieces, size, width), bf16)] * 5 + [
-        dma((5,)),
-        dma((steps,)),
-        dma((steps,)),
-        dma((2, 2 * pieces)),
-        dma((2, 1)),
-        dma((2, steps)),
-        dma((2, 1)),
-        dma((2, steps)),
-        dma((2, 2 * steps)),
-        dma((2, steps)),
-        dma((2, steps)),
-        dma((2, steps)),
-        dma((2, steps)),
-        dma((2, steps)),
-        dma((2, 2 * pieces)),
-        dma((2, 2 * pieces)),
-        dma((2, 2 * pieces)),
-        dma((2, 2 * pieces)),
-        dma((2, pieces)),
+    ] + [vmem((rows, width), bf16)] * 5 + [
+        dma((7,)),
+        dma((9,)),
+        dma((max(2 * groups, groups + 2 * steps),)),
+        dma((max(2 * groups, 2 * steps),)),
+        dma((2 * groups,)),
+        dma((groups,)),
+        dma((min(groups, 3),)),
+        dma((4,)),
     ]
     in_vmem = pl.BlockSpec(memory_space=pltpu.VMEM)
     in_hbm = pl.BlockSpec(memory_space=pltpu.HBM)

time: 38.8 us -> 35.3 us (0.910)
  Pallas kernels: 38 us -> 34.5 us
    pallas_call x1, Pallas kernels: 35 us -> 31.5 us  [fused(): pl.pallas_call(functools.partial(window, islands, pieces, splits, float(d...]
where the time goes in v2:
time: 35.3 us; the launch traced here: 35.2 us
  Pallas kernels  34.5 us (98%)
  between operations  0.64 us (2%)
    pallas_call x1, Pallas kernels, fused(): pl.pallas_call(functools.partial(window, islands, pieces, splits, float(d...  31.5 us
    pallas_call x1, Pallas kernels, fused(): pl.pallas_call(write_back, out_shape=out_shape, in_specs=[in_vmem] * len(...  3.07 us

profile of v2, /device:TPU:1, one launch (start us, length us, event | category | flops | bytes accessed | tf_op | source)
XLA Modules:
  0.0 35.2 jit_solution(3204458677591118035)
XLA Ops:
  0.6 31.5 %shard_map.110 = (bf16[1024,512]{1,0:T(8,128)(2,1)S(1)}, bf16[1024,512]{1,0:T(8,128)(2,1)S(1)}, bf16[1024,512]{1,0:T(8,128)(2,1)S(1)}, f32[1024,512]{1,0:T(8,128)S(1)}, f32[1024,512]{1,0:T(8,128)S(1)}) custom-call(bf16[1024,512]{1,0:T(8,128)(2,1)} %bitcast.8, bf16[1024,512]{1,0:T(8,128)(2,1)} %bitcast.9, bf16[1024,512]{1,0:T(8,128)(2,1)} %bitcast.10, ...), custom_call_target="tpu_custom_call" | custom-call | tf_op jit(solution)/shard_map/pallas_call | solution.py:790
  32.1 3.1 %shard_map.111 = (bf16[1024,512]{1,0:T(8,128)(2,1)}, bf16[1024,512]{1,0:T(8,128)(2,1)}, bf16[1024,512]{1,0:T(8,128)(2,1)}, f32[1024,512]{1,0:T(8,128)}, f32[1024,512]{1,0:T(8,128)}) custom-call(bf16[1024,512]{1,0:T(8,128)(2,1)S(1)} %get-tuple-element.15.refs_0_, bf16[1024,512]{1,0:T(8,128)(2,1)S(1)} %get-tuple-element.16.refs_1_, ...), custom_call_target="tpu_custom_call" | custom-call | tf_op jit(solution)/shard_map/pallas_call | solution.py:800

commit v3 on v2

--- a/solution.py
+++ b/solution.py
@@ -268,10 +268,10 @@
 
 def window(islands, pieces, splits, scale, *refs):
     w_hbm, m_hbm, s_hbm, gw_hbm, om_hbm, x_hbm, cot_hbm = refs[:7]
-    nl, nf, ns, ng, nm = refs[7:12]
-    (wc, xc, xin, cot, own, psend, precv, kg, kgin, grad, half_inner, m, s, gw, om, mean,
+    nf, ns, half_inner, mean, gw, om = refs[7:13]
+    (wc, xc, xin, cot, own, psend, precv, kg, kgin, grad, m, s,
      rsin, pin, qin, pout, res,
-     load_sem, sent, first, rail, cross, gathered, kept_sem, passed) = refs[12:]
+     load_sem, sent, first, rail, cross, gathered, kept_sem, passed) = refs[13:]
     rows, width = mean.shape
     half = rows // 2
     groups = range(len(pieces))
@@ -525,28 +525,6 @@
         @pl.loop(0, rows // tile)
         def _(t):
             gradient_tile(base, pl.multiple_of(t * tile, tile), tile)
-
-    def outer_update(start, extent):
-        step = 32 if extent % 32 == 0 else 16
-
-        @pl.loop(0, extent // step)
-        def _(u):
-            place = pl.ds(pl.multiple_of(start + u * step, step), step)
-            weights = gw[place, :]
-            outer_grad = weights - mean[place, :].astype(f32)
-            momentum = outer_beta * om[place, :] + outer_grad
-            updated = weights - outer_rate * (outer_grad + outer_beta * momentum)
-            nm[place, :] = momentum
-            ng[place, :] = updated
-
-    def merge(start, extent):
-        step = 32 if extent % 32 == 0 else 16
-
-        @pl.loop(0, extent // step)
-        def _(u):
-            place = pl.ds(pl.multiple_of(start + u * step, step), step)
-            nl[place, :] = (
-                half_inner[place, :] + (1.0 - merge_weight) * ng[place, :]).astype(bf16)
 
     def matmul(out, place, left, convert):
         part = min(256, width)
@@ -606,11 +584,7 @@
         inner_update(0)
         for j in groups:
             deliver_send(j).wait_recv()
-            outer_update(kept(j), pieces[j])
-            merge(kept(j), pieces[j])
             gather_recv(j).wait_recv()
-            outer_update(given(j), pieces[j])
-            merge(given(j), pieces[j])
         for total in (scatter_total(), token_total(), keep_total(), own_tokens_up_total(),
                       tokens_forward(every), partial_send(every, 0), upstream_across(every, 0),
                       upstream_down(every), upstream_forward(every)):
@@ -628,7 +602,6 @@
             j = k // 2
             if k % 2:
                 mean[kept_rows(j), :] = res[slot(k), :]
-                outer_update(kept(j), pieces[j])
             else:
                 deliver_send(j).start()
 
@@ -643,8 +616,6 @@
         for load in state_loads:
             load.start()
         wload.wait()
-        state_loads[2].wait()
-        state_loads[3].wait()
 
         def arrived(k):
             scatter_send(k % 2, k // 2).wait_recv()
@@ -685,39 +656,52 @@
         def gradient_ready():
             tokens_forward(every).wait_recv()
             upstream_forward(every).wait_recv()
-            for load in state_loads[:2]:
+            for load in state_loads:
                 load.wait()
 
+        ends = [2 * begins[k // 2] + (1 + k % 2) * pieces[k // 2] for k in range(count)]
+
         def interleave(first, second, lag, own_at, tiles_at):
-            work = {}
-            work.setdefault(min(own_at, count - 1), []).append(gradient_start)
-            for t in range(tiles):
-                place = work.setdefault(min(tiles_at + t, count - 1), [])
-                if t == 0:
-                    place.append(gradient_ready)
-                place.append(functools.partial(gradient_tile, rows, t * tile, tile))
+            work = []
+            if own_at < 16:
+                work.append((own_at * rows // 16, gradient_start))
+                work.append((tiles_at * rows // 16, gradient_ready))
+                for t in range(tiles):
+                    work.append(((tiles_at + t) * rows // 16, functools.partial(
+                        gradient_tile, rows, t * tile, tile)))
             done = 0
-            for k in range(count + lag):
+            for k in range(count + 1):
                 if k < count:
                     first(k)
-                if k >= lag:
-                    second(k - lag)
-                    for item in work.get(k - lag, ()):
-                        item()
+                limit = rows * 2 if k == count else ends[k] - lag * rows // 16
+                while done < count and ends[done] <= limit:
+                    second(done)
+                    while work and work[0][0] <= ends[done]:
+                        work.pop(0)[1]()
+                    done += 1
+            for item in work:
+                item[1]()
 
         @pl.when(inside == 0)
         def _():
-            interleave(outer_part, outer_result, count, count * 10 // 16, count * 14 // 16)
+            interleave(outer_part, outer_result, 16, 11, 15)
+
+        @pl.when(level == 1)
+        def _():
+            interleave(middle_part, middle_result, 4, 16, 16)
+
+        @pl.when(level == 2)
+        def _():
+            interleave(middle_part, middle_result, 4, 16, 16)
 
         @pl.when(inside == 1)
         def _():
-            interleave(middle_part, middle_result, min(4, count), count, count)
-
-        merge(pl.multiple_of(side * half, half), half)
+            gradient_start()
+            gradient_ready()
+            inner_update(rows)
+
         for j in groups:
             gather_recv(j).wait_recv()
-            outer_update(given(j), pieces[j])
-            merge(given(j), pieces[j])
 
         @pl.when(inside == 1)
         def _():
@@ -728,20 +712,35 @@
             total.wait_send()
 
 
-def write_back(*refs):
-    arrays = len(refs) // 2
-    sems = refs[-1]
-    copies = []
-    for index in range(arrays):
-        part = refs[index].shape[0] // 2
-        for piece in range(2):
-            place = pl.ds(piece * part, part)
-            copies.append(pltpu.make_async_copy(
-                refs[index].at[place], refs[arrays + index].at[place], sems.at[index, piece]))
-    for copy in copies:
-        copy.start()
-    for copy in copies:
-        copy.wait()
+def finish(first, second, half_inner, mean, gw, om, nl, nf, ns, ng, nm, local, weights, momenta,
+           sems):
+    rows = mean.shape[0]
+    tile = min(128, rows)
+    step = min(32, tile)
+    f32 = jnp.float32
+    pltpu.make_async_copy(first, nf, sems.at[0]).start()
+    pltpu.make_async_copy(second, ns, sems.at[1]).start()
+    results = ((local, nl, sems.at[2]), (weights, ng, sems.at[3]), (momenta, nm, sems.at[4]))
+    for t in range(rows // tile):
+        @pl.loop(0, tile // step)
+        def _(u):
+            place = pl.ds(pl.multiple_of(t * tile + u * step, step), step)
+            current = gw[place, :]
+            outer_grad = current - mean[place, :].astype(f32)
+            momentum = outer_beta * om[place, :] + outer_grad
+            updated = current - outer_rate * (outer_grad + outer_beta * momentum)
+            momenta[place, :] = momentum
+            weights[place, :] = updated
+            local[place, :] = (
+                half_inner[place, :] + (1.0 - merge_weight) * updated).astype(jnp.bfloat16)
+
+        part = pl.ds(t * tile, tile)
+        for source, target, sem in results:
+            pltpu.make_async_copy(source.at[part], target.at[part], sem).start()
+    pltpu.make_async_copy(first, nf, sems.at[0]).wait()
+    pltpu.make_async_copy(second, ns, sems.at[1]).wait()
+    for source, target, sem in results:
+        pltpu.make_async_copy(source, target, sem).wait()
 
 
 def fused(pieces, local_weights, adam_first, adam_second, global_weights, outer_momentum, inputs,
@@ -755,8 +754,10 @@
     groups = len(pieces)
     bf16, f32 = jnp.bfloat16, jnp.float32
     dma, vmem = pltpu.SemaphoreType.DMA, pltpu.VMEM
-    out_shape = [jax.ShapeDtypeStruct((rows, width), bf16)] * 3 + [
-        jax.ShapeDtypeStruct((rows, width), f32)] * 2
+    narrow = jax.ShapeDtypeStruct((rows, width), bf16)
+    wide = jax.ShapeDtypeStruct((rows, width), f32)
+    carried = [narrow, narrow, wide, narrow, wide, wide]
+    out_shape = [narrow] * 3 + [wide] * 2
     steps = len(splits)
     scratch = [
         vmem((2 * rows, width), bf16),
@@ -769,11 +770,7 @@
         vmem((2 * count, width), bf16),
         vmem((2 * count, width), bf16),
         vmem((rows, width), f32),
-        vmem((rows, width), f32),
         vmem((rows, width), bf16),
-        vmem((rows, width), bf16),
-        vmem((rows, width), f32),
-        vmem((rows, width), f32),
         vmem((rows, width), bf16),
     ] + [vmem((rows, width), bf16)] * 5 + [
         dma((7,)),
@@ -789,21 +786,26 @@
     in_hbm = pl.BlockSpec(memory_space=pltpu.HBM)
     results = pl.pallas_call(
         functools.partial(window, islands, pieces, splits, float(depth) ** (-0.5)),
-        out_shape=out_shape,
+        out_shape=carried,
         in_specs=[in_hbm] * len(arrays),
-        out_specs=[in_vmem] * len(out_shape),
+        out_specs=[in_vmem] * len(carried),
         scratch_shapes=scratch,
         compiler_params=pltpu.CompilerParams(
             collective_id=0, has_side_effects=True, vmem_limit_bytes=40 * 1024 * 1024
         ),
     )(*(pltpu.with_memory_space_constraint(a, pltpu.HBM) for a in arrays))
     written = pl.pallas_call(
-        write_back,
+        finish,
         out_shape=out_shape,
-        in_specs=[in_vmem] * len(out_shape),
+        in_specs=[in_vmem] * len(carried),
         out_specs=[in_hbm] * len(out_shape),
-        scratch_shapes=[dma((len(out_shape), 2))],
-        compiler_params=pltpu.CompilerParams(vmem_limit_bytes=4 * 1024 * 1024),
+        scratch_shapes=[
+            vmem((rows, width), bf16),
+            vmem((rows, width), f32),
+            vmem((rows, width), f32),
+            dma((len(out_shape),)),
+        ],
+        compiler_params=pltpu.CompilerParams(vmem_limit_bytes=8 * 1024 * 1024),
     )(*results)
     return tuple(a[None] for a in written[:3]) + tuple(written[3:])
 

time: 35.3 us -> 34.4 us (0.975)
  Pallas kernels: 34.5 us -> 33.6 us
    pallas_call x1, Pallas kernels: 31.5 us -> 30.6 us  [fused(): pl.pallas_call(functools.partial(window, islands, pieces, splits, float(d...]
where the time goes in v3:
time: 34.4 us; the launch traced here: 34.2 us
  Pallas kernels  33.6 us (98%)
  between operations  0.64 us (2%)
    pallas_call x1, Pallas kernels, fused(): pl.pallas_call(functools.partial(window, islands, pieces, splits, float(d...  30.6 us
    pallas_call x1, Pallas kernels, fused(): pl.pallas_call(finish, out_shape=out_shape, in_specs=[in_vmem] * len(carr...  2.99 us

profile of v3, /device:TPU:1, one launch (start us, length us, event | category | flops | bytes accessed | tf_op | source)
XLA Modules:
  0.0 34.2 jit_solution(12468477141282666606)
XLA Ops:
  0.6 30.6 %shard_map.110 = (bf16[1024,512]{1,0:T(8,128)(2,1)S(1)}, bf16[1024,512]{1,0:T(8,128)(2,1)S(1)}, f32[1024,512]{1,0:T(8,128)S(1)}, bf16[1024,512]{1,0:T(8,128)(2,1...) custom-call(bf16[1024,512]{1,0:T(8,128)(2,1)} %bitcast.8, bf16[1024,512]{1,0:T(8,128)(2,1)} %bitcast.9, ...), custom_call_target="tpu_custom_call" | custom-call | tf_op jit(solution)/shard_map/pallas_call | solution.py:787
  31.2 3.0 %shard_map.111 = (bf16[1024,512]{1,0:T(8,128)(2,1)}, bf16[1024,512]{1,0:T(8,128)(2,1)}, bf16[1024,512]{1,0:T(8,128)(2,1)}, f32[1024,512]{1,0:T(8,128)}, f32[1024,512]{1,0:T(8,128)}) custom-call(bf16[1024,512]{1,0:T(8,128)(2,1)S(1)} %get-tuple-element.16.first, bf16[1024,512]{1,0:T(8,128)(2,1)S(1)} %get-tuple-element.17.second, ...), custom_call_target="tpu_custom_call" | custom-call | tf_op jit(solution)/shard_map/pallas_call | solution.py:797

commit v4 on v3

--- a/solution.py
+++ b/solution.py
@@ -266,12 +266,21 @@
     return ()
 
 
+def inner_step(gradient, first, second, current):
+    first_new = beta_one * first.astype(jnp.float32) + (1.0 - beta_one) * gradient
+    second_new = beta_two * second.astype(jnp.float32) + (1.0 - beta_two) * gradient * gradient
+    current = current.astype(jnp.float32)
+    inner = current - inner_rate * (
+        first_new / (jnp.sqrt(second_new) + adam_epsilon) + weight_decay * current)
+    return first_new.astype(jnp.bfloat16), second_new.astype(jnp.bfloat16), merge_weight * inner
+
+
 def window(islands, pieces, splits, scale, *refs):
     w_hbm, m_hbm, s_hbm, gw_hbm, om_hbm, x_hbm, cot_hbm = refs[:7]
-    nf, ns, half_inner, mean, gw, om = refs[7:13]
-    (wc, xc, xin, cot, own, psend, precv, kg, kgin, grad, m, s,
+    nf, ns, half_inner, mean, gw, om, grad, m, s, late = refs[7:17]
+    (wc, xc, xin, cot, own, psend, precv, kg, kgin, xct, xint,
      rsin, pin, qin, pout, res,
-     load_sem, sent, first, rail, cross, gathered, kept_sem, passed) = refs[13:]
+     load_sem, sent, first, rail, cross, gathered, kept_sem, passed, ready) = refs[17:]
     rows, width = mean.shape
     half = rows // 2
     groups = range(len(pieces))
@@ -323,9 +332,12 @@
 
     greet(partner)
     greet(beside(1))
-    greet(across(0))
-
-    @pl.when(core == 0)
+
+    @pl.when(chip == 0)
+    def _():
+        greet(across(0))
+
+    @pl.when((core == 0) & (chip == 0))
     def _():
         greet(across(1))
 
@@ -351,7 +363,17 @@
     for load in tokens:
         load.start()
 
-    pl.semaphore_wait(barrier, 4 + core * (1 + inside))
+    pl.semaphore_wait(barrier, 4 + core * (1 + inside) - (1 - chip) * (2 - core))
+
+    @pl.when((core == 0) & (chip == 1))
+    def _():
+        for c in range(2):
+            pl.semaphore_signal(ready, inc=1, device_id=across(c), device_id_type=MESH)
+
+    def reach_across():
+        @pl.when(chip == 0)
+        def _():
+            pl.semaphore_wait(ready, 1)
 
     def remote(src, dst, kind, into, target):
         return pltpu.make_async_remote_copy(
@@ -486,45 +508,51 @@
 
     state_loads = [
         pltpu.make_async_copy(place, dst, load_sem.at[3 + index])
-        for index, (place, dst) in enumerate(((m_hbm, m), (s_hbm, s), (gw_hbm, gw), (om_hbm, om)))
+        for index, (place, dst) in enumerate((
+            (m_hbm, m), (s_hbm, s), (gw_hbm, gw), (om_hbm, om),
+            (w_hbm.at[pl.ds(rows - late.shape[0], late.shape[0])], late)))
     ]
 
-    def own_gradient(base):
+    def turn(out, tokens_by_width, base, start, tile):
+        columns = pl.ds(pl.multiple_of(base + start, tile), tile)
+        out[pl.ds(start, tile), :] = tokens_by_width[:, columns].T
+
+    def turn_all(out, tokens_by_width, base):
         tile = min(256, rows)
 
         @pl.loop(0, rows // tile)
         def _(t):
-            start = pl.multiple_of(t * tile, tile)
-            grad[pl.ds(start, tile), :] = lax.dot_general(
-                xc[:, pl.ds(pl.multiple_of(base + start, tile), tile)], kg[...],
-                (((0,), (0,)), ((), ())), preferred_element_type=f32)
+            turn(out, tokens_by_width, base, pl.multiple_of(t * tile, tile), tile)
+
+    def own_gradient():
+        tile = min(256, rows)
+
+        @pl.loop(0, rows // tile)
+        def _(t):
+            place = pl.ds(pl.multiple_of(t * tile, tile), tile)
+            grad[place, :] = jnp.dot(xct[place, :], kg[...], preferred_element_type=f32)
 
     def gradient_tile(base, start, tile):
-        grad[pl.ds(start, tile), :] += lax.dot_general(
-            xin[:, pl.ds(pl.multiple_of(base + start, tile), tile)], kgin[...],
-            (((0,), (0,)), ((), ())), preferred_element_type=f32)
+        place = pl.ds(start, tile)
+        grad[place, :] += jnp.dot(xint[place, :], kgin[...], preferred_element_type=f32)
+        if start >= nf.shape[0]:
+            return
         step = min(32, tile)
 
         @pl.loop(0, tile // step)
         def _(u):
             place = pl.ds(pl.multiple_of(start + u * step, step), step)
-            gradient = grad[place, :]
-            first_new = beta_one * m[place, :].astype(f32) + (1.0 - beta_one) * gradient
-            second_new = (
-                beta_two * s[place, :].astype(f32) + (1.0 - beta_two) * gradient * gradient)
-            nf[place, :] = first_new.astype(bf16)
-            ns[place, :] = second_new.astype(bf16)
-            current = wc[pl.ds(pl.multiple_of(base + start + u * step, step), step), :].astype(f32)
-            inner = current - inner_rate * (
-                first_new / (jnp.sqrt(second_new) + adam_epsilon) + weight_decay * current)
-            half_inner[place, :] = merge_weight * inner
+            current = wc[pl.ds(pl.multiple_of(base + start + u * step, step), step), :]
+            first_new, second_new, inner = inner_step(
+                grad[place, :], m[place, :], s[place, :], current)
+            nf[place, :] = first_new
+            ns[place, :] = second_new
+            half_inner[place, :] = inner
 
     def inner_update(base):
         tile = min(256, rows)
-
-        @pl.loop(0, rows // tile)
-        def _(t):
-            gradient_tile(base, pl.multiple_of(t * tile, tile), tile)
+        for t in range(rows // tile):
+            gradient_tile(base, t * tile, tile)
 
     def matmul(out, place, left, convert):
         part = min(256, width)
@@ -545,17 +573,19 @@
             scatter_send(0, j).start()
             if j < 3:
                 keep_send(j).start()
-            if j < 2 and j < parts:
-                token_send(0, j).start()
         for i in steps:
             own_tokens_up(i).start()
         for load in state_loads:
             load.start()
+        reach_across()
+        for i in steps[:2]:
+            token_send(0, i).start()
         wload.wait()
         tokens_loaded()
         weight_send.wait_recv()
         own_tokens_down_total().wait_recv()
         matmul(own, every, xc, False)
+        turn_all(xct, xc, 0)
         for i in steps:
             token_send(0, i).wait_recv()
             token_send(1, i).wait_recv()
@@ -575,7 +605,8 @@
                     keys, cot[both(i), columns].astype(f32), scale)
             upstream_across(both(i), i).start()
             upstream_down(both(i)).start()
-        own_gradient(0)
+        own_gradient()
+        turn_all(xint, xin, 0)
         for i in steps:
             upstream_across(both(i), i).wait_recv()
             upstream_forward(both(i)).start()
@@ -607,14 +638,15 @@
 
         for j in groups:
             scatter_send(1, j).start()
-            if j < parts:
-                token_send(1, j).start()
         weight_send.start()
         for i in steps:
             own_tokens_down(i).start()
             cotangent_down(i).start()
         for load in state_loads:
             load.start()
+        reach_across()
+        for i in steps:
+            token_send(1, i).start()
         wload.wait()
 
         def arrived(k):
@@ -647,28 +679,33 @@
         tile = min(256, rows)
         tiles = rows // tile
 
-        def gradient_start():
+        def own_tokens_ready():
             tokens_loaded()
             own_tokens_up_total().wait_recv()
+
+        def gradient_start():
             upstream_down(every).wait_recv()
-            own_gradient(rows)
+            own_gradient()
 
         def gradient_ready():
-            tokens_forward(every).wait_recv()
             upstream_forward(every).wait_recv()
             for load in state_loads:
                 load.wait()
 
         ends = [2 * begins[k // 2] + (1 + k % 2) * pieces[k // 2] for k in range(count)]
 
-        def interleave(first, second, lag, own_at, tiles_at):
+        def interleave(first, second, lag, turn_at, own_at, tiles_at):
+            unit = rows // 16
             work = []
-            if own_at < 16:
-                work.append((own_at * rows // 16, gradient_start))
-                work.append((tiles_at * rows // 16, gradient_ready))
-                for t in range(tiles):
-                    work.append(((tiles_at + t) * rows // 16, functools.partial(
-                        gradient_tile, rows, t * tile, tile)))
+            work.append((turn_at * unit, tokens_forward(every).wait_recv))
+            for t in range(tiles):
+                work.append(((turn_at + t) * unit, functools.partial(
+                    turn, xint, xin, rows, t * tile, tile)))
+            work.append((own_at * unit, gradient_start))
+            work.append((tiles_at * unit, gradient_ready))
+            for t in range(tiles):
+                work.append(((tiles_at + t) * unit, functools.partial(
+                    gradient_tile, rows, t * tile, tile)))
             done = 0
             for k in range(count + 1):
                 if k < count:
@@ -682,23 +719,16 @@
             for item in work:
                 item[1]()
 
+        own_tokens_ready()
+        turn_all(xct, xc, rows)
+
         @pl.when(inside == 0)
         def _():
-            interleave(outer_part, outer_result, 16, 11, 15)
-
-        @pl.when(level == 1)
-        def _():
-            interleave(middle_part, middle_result, 4, 16, 16)
-
-        @pl.when(level == 2)
-        def _():
-            interleave(middle_part, middle_result, 4, 16, 16)
+            interleave(outer_part, outer_result, 16, 14, 14, 16)
 
         @pl.when(inside == 1)
         def _():
-            gradient_start()
-            gradient_ready()
-            inner_update(rows)
+            interleave(middle_part, middle_result, 4, 16, 16, 16)
 
         for j in groups:
             gather_recv(j).wait_recv()
@@ -712,35 +742,54 @@
             total.wait_send()
 
 
-def finish(first, second, half_inner, mean, gw, om, nl, nf, ns, ng, nm, local, weights, momenta,
-           sems):
+def finish(first, second, half_inner, mean, gw, om, grad, m, s, late, nl, nf, ns, ng, nm, local,
+           weights, momenta, first_late, second_late, sems):
     rows = mean.shape[0]
-    tile = min(128, rows)
+    early = first.shape[0]
+    tile = min(128, early)
     step = min(32, tile)
     f32 = jnp.float32
-    pltpu.make_async_copy(first, nf, sems.at[0]).start()
-    pltpu.make_async_copy(second, ns, sems.at[1]).start()
-    results = ((local, nl, sems.at[2]), (weights, ng, sems.at[3]), (momenta, nm, sems.at[4]))
+    begin = pl.ds(0, early)
+    rest = pl.ds(early, rows - early)
+    pltpu.make_async_copy(first, nf.at[begin], sems.at[0]).start()
+    pltpu.make_async_copy(second, ns.at[begin], sems.at[1]).start()
     for t in range(rows // tile):
+        after = t * tile - early
+
         @pl.loop(0, tile // step)
         def _(u):
             place = pl.ds(pl.multiple_of(t * tile + u * step, step), step)
+            if after < 0:
+                inner = half_inner[place, :]
+            else:
+                behind = pl.ds(pl.multiple_of(after + u * step, step), step)
+                first_new, second_new, inner = inner_step(
+                    grad[place, :], m[place, :], s[place, :], late[behind, :])
+                first_late[behind, :] = first_new
+                second_late[behind, :] = second_new
             current = gw[place, :]
             outer_grad = current - mean[place, :].astype(f32)
             momentum = outer_beta * om[place, :] + outer_grad
             updated = current - outer_rate * (outer_grad + outer_beta * momentum)
             momenta[place, :] = momentum
             weights[place, :] = updated
-            local[place, :] = (
-                half_inner[place, :] + (1.0 - merge_weight) * updated).astype(jnp.bfloat16)
+            local[place, :] = (inner + (1.0 - merge_weight) * updated).astype(jnp.bfloat16)
 
         part = pl.ds(t * tile, tile)
-        for source, target, sem in results:
-            pltpu.make_async_copy(source.at[part], target.at[part], sem).start()
-    pltpu.make_async_copy(first, nf, sems.at[0]).wait()
-    pltpu.make_async_copy(second, ns, sems.at[1]).wait()
-    for source, target, sem in results:
-        pltpu.make_async_copy(source, target, sem).wait()
+        if after >= 0:
+            behind = pl.ds(after, tile)
+            pltpu.make_async_copy(first_late.at[behind], nf.at[part], sems.at[5]).start()
+            pltpu.make_async_copy(second_late.at[behind], ns.at[part], sems.at[6]).start()
+        pltpu.make_async_copy(local.at[part], nl.at[part], sems.at[2]).start()
+        pltpu.make_async_copy(weights.at[part], ng.at[part], sems.at[3]).start()
+        pltpu.make_async_copy(momenta.at[part], nm.at[part], sems.at[4]).start()
+    pltpu.make_async_copy(first, nf.at[begin], sems.at[0]).wait()
+    pltpu.make_async_copy(second, ns.at[begin], sems.at[1]).wait()
+    pltpu.make_async_copy(local, nl, sems.at[2]).wait()
+    pltpu.make_async_copy(weights, ng, sems.at[3]).wait()
+    pltpu.make_async_copy(momenta, nm, sems.at[4]).wait()
+    pltpu.make_async_copy(first_late, nf.at[rest], sems.at[5]).wait()
+    pltpu.make_async_copy(second_late, ns.at[rest], sems.at[6]).wait()
 
 
 def fused(pieces, local_weights, adam_first, adam_second, global_weights, outer_momentum, inputs,
@@ -756,7 +805,10 @@
     dma, vmem = pltpu.SemaphoreType.DMA, pltpu.VMEM
     narrow = jax.ShapeDtypeStruct((rows, width), bf16)
     wide = jax.ShapeDtypeStruct((rows, width), f32)
-    carried = [narrow, narrow, wide, narrow, wide, wide]
+    early = rows // 2
+    part = jax.ShapeDtypeStruct((early, width), bf16)
+    carried = [part, part, jax.ShapeDtypeStruct((early, width), f32), narrow, wide, wide, wide,
+               narrow, narrow, jax.ShapeDtypeStruct((rows - early, width), bf16)]
     out_shape = [narrow] * 3 + [wide] * 2
     steps = len(splits)
     scratch = [
@@ -769,11 +821,10 @@
         vmem((2 * count, width), bf16),
         vmem((2 * count, width), bf16),
         vmem((2 * count, width), bf16),
-        vmem((rows, width), f32),
-        vmem((rows, width), bf16),
-        vmem((rows, width), bf16),
+        vmem((rows, 2 * count), bf16),
+        vmem((rows, 2 * count), bf16),
     ] + [vmem((rows, width), bf16)] * 5 + [
-        dma((7,)),
+        dma((8,)),
         dma((9,)),
         dma((max(2 * groups, groups + 2 * steps),)),
         dma((max(2 * groups, 2 * steps),)),
@@ -781,6 +832,7 @@
         dma((groups,)),
         dma((min(groups, 3),)),
         dma((4,)),
+        pltpu.SemaphoreType.REGULAR,
     ]
     in_vmem = pl.BlockSpec(memory_space=pltpu.VMEM)
     in_hbm = pl.BlockSpec(memory_space=pltpu.HBM)
@@ -803,7 +855,9 @@
             vmem((rows, width), bf16),
             vmem((rows, width), f32),
             vmem((rows, width), f32),
-            dma((len(out_shape),)),
+            vmem((rows - early, width), bf16),
+            vmem((rows - early, width), bf16),
+            dma((7,)),
         ],
         compiler_params=pltpu.CompilerParams(vmem_limit_bytes=8 * 1024 * 1024),
     )(*results)

time: 34.4 us -> 33.6 us (0.977)
  Pallas kernels: 33.6 us -> 32.8 us
    pallas_call x1, Pallas kernels: 30.6 us -> 29.8 us  [fused(): pl.pallas_call(functools.partial(window, islands, pieces, splits, float(d...]
where the time goes in v4:
time: 33.6 us; the launch traced here: 33.4 us
  Pallas kernels  32.8 us (98%)
  between operations  0.64 us (2%)
    pallas_call x1, Pallas kernels, fused(): pl.pallas_call(functools.partial(window, islands, pieces, splits, float(d...  29.8 us
    pallas_call x1, Pallas kernels, fused(): pl.pallas_call(finish, out_shape=out_shape, in_specs=[in_vmem] * len(carr...  3.01 us

profile of v4, /device:TPU:1, one launch (start us, length us, event | category | flops | bytes accessed | tf_op | source)
XLA Modules:
  0.0 33.4 jit_solution(94231594615513096)
XLA Ops:
  0.6 29.8 %shard_map.110 = (bf16[512,512]{1,0:T(8,128)(2,1)S(1)}, bf16[512,512]{1,0:T(8,128)(2,1)S(1)}, f32[512,512]{1,0:T(8,128)S(1)}, bf16[1024,512]{1,0:T(8,128)(2,1)S(...) custom-call(bf16[1024,512]{1,0:T(8,128)(2,1)} %bitcast.8, ...), custom_call_target="tpu_custom_call" | custom-call | tf_op jit(solution)/shard_map/pallas_call | solution.py:839
  30.4 3.0 %shard_map.111 = (bf16[1024,512]{1,0:T(8,128)(2,1)}, bf16[1024,512]{1,0:T(8,128)(2,1)}, bf16[1024,512]{1,0:T(8,128)(2,1)}, f32[1024,512]{1,0:T(8,128)}, f32[1024,512]{1,0:T(8,128)}) custom-call(bf16[512,512]{1,0:T(8,128)(2,1)S(1)} %get-tuple-element.20.first, bf16[512,512]{1,0:T(8,128)(2,1)S(1)} %get-tuple-element.21.second, ...), custom_call_target="tpu_custom_call" | custom-call | tf_op jit(solution)/shard_map/pallas_call | solution.py:849

commit v5 on v4

--- a/solution.py
+++ b/solution.py
@@ -701,6 +701,10 @@
             for t in range(tiles):
                 work.append(((turn_at + t) * unit, functools.partial(
                     turn, xint, xin, rows, t * tile, tile)))
+            work.append((turn_at * unit, own_tokens_ready))
+            for t in range(tiles):
+                work.append(((turn_at + t) * unit, functools.partial(
+                    turn, xct, xc, rows, t * tile, tile)))
             work.append((own_at * unit, gradient_start))
             work.append((tiles_at * unit, gradient_ready))
             for t in range(tiles):
@@ -718,9 +722,6 @@
                     done += 1
             for item in work:
                 item[1]()
-
-        own_tokens_ready()
-        turn_all(xct, xc, rows)
 
         @pl.when(inside == 0)
         def _():

time: 33.6 us -> 33.6 us (level)
  no operation moved by 1% of the time
where the time goes in v5:
time: 33.6 us; the launch traced here: 33.4 us
  Pallas kernels  32.8 us (98%)
  between operations  0.64 us (2%)
    pallas_call x1, Pallas kernels, fused(): pl.pallas_call(functools.partial(window, islands, pieces, splits, float(d...  29.8 us
    pallas_call x1, Pallas kernels, fused(): pl.pallas_call(finish, out_shape=out_shape, in_specs=[in_vmem] * len(carr...  3.01 us

profile of v5, /device:TPU:1, one launch (start us, length us, event | category | flops | bytes accessed | tf_op | source)
XLA Modules:
  0.0 33.4 jit_solution(10900434814839310620)
XLA Ops:
  0.6 29.8 %shard_map.110 = (bf16[512,512]{1,0:T(8,128)(2,1)S(1)}, bf16[512,512]{1,0:T(8,128)(2,1)S(1)}, f32[512,512]{1,0:T(8,128)S(1)}, bf16[1024,512]{1,0:T(8,128)(2,1)S(...) custom-call(bf16[1024,512]{1,0:T(8,128)(2,1)} %bitcast.8, ...), custom_call_target="tpu_custom_call" | custom-call | tf_op jit(solution)/shard_map/pallas_call | solution.py:840
  30.4 3.0 %shard_map.111 = (bf16[1024,512]{1,0:T(8,128)(2,1)}, bf16[1024,512]{1,0:T(8,128)(2,1)}, bf16[1024,512]{1,0:T(8,128)(2,1)}, f32[1024,512]{1,0:T(8,128)}, f32[1024,512]{1,0:T(8,128)}) custom-call(bf16[512,512]{1,0:T(8,128)(2,1)S(1)} %get-tuple-element.20.first, bf16[512,512]{1,0:T(8,128)(2,1)S(1)} %get-tuple-element.21.second, ...), custom_call_target="tpu_custom_call" | custom-call | tf_op jit(solution)/shard_map/pallas_call | solution.py:850

commit v6 on v5

--- a/solution.py
+++ b/solution.py
@@ -806,7 +806,7 @@
     dma, vmem = pltpu.SemaphoreType.DMA, pltpu.VMEM
     narrow = jax.ShapeDtypeStruct((rows, width), bf16)
     wide = jax.ShapeDtypeStruct((rows, width), f32)
-    early = rows // 2
+    early = rows // 4
     part = jax.ShapeDtypeStruct((early, width), bf16)
     carried = [part, part, jax.ShapeDtypeStruct((early, width), f32), narrow, wide, wide, wide,
                narrow, narrow, jax.ShapeDtypeStruct((rows - early, width), bf16)]

time: 33.6 us -> 33.8 us (level)
  no operation moved by 1% of the time
where the time goes in v6:
time: 33.8 us; the launch traced here: 33.7 us
  Pallas kernels  33 us (98%)
  between operations  0.64 us (2%)
    pallas_call x1, Pallas kernels, fused(): pl.pallas_call(functools.partial(window, islands, pieces, splits, float(d...  29.8 us
    pallas_call x1, Pallas kernels, fused(): pl.pallas_call(finish, out_shape=out_shape, in_specs=[in_vmem] * len(carr...  3.25 us

profile of v6, /device:TPU:1, one launch (start us, length us, event | category | flops | bytes accessed | tf_op | source)
XLA Modules:
  0.0 33.7 jit_solution(13735561529081610398)
XLA Ops:
  0.6 29.8 %shard_map.110 = (bf16[256,512]{1,0:T(8,128)(2,1)S(1)}, bf16[256,512]{1,0:T(8,128)(2,1)S(1)}, f32[256,512]{1,0:T(8,128)S(1)}, bf16[1024,512]{1,0:T(8,128)(2,1)S(...) custom-call(bf16[1024,512]{1,0:T(8,128)(2,1)} %bitcast.8, ...), custom_call_target="tpu_custom_call" | custom-call | tf_op jit(solution)/shard_map/pallas_call | solution.py:840
  30.4 3.3 %shard_map.111 = (bf16[1024,512]{1,0:T(8,128)(2,1)}, bf16[1024,512]{1,0:T(8,128)(2,1)}, bf16[1024,512]{1,0:T(8,128)(2,1)}, f32[1024,512]{1,0:T(8,128)}, f32[1024,512]{1,0:T(8,128)}) custom-call(bf16[256,512]{1,0:T(8,128)(2,1)S(1)} %get-tuple-element.20.first, bf16[256,512]{1,0:T(8,128)(2,1)S(1)} %get-tuple-element.21.second, ...), custom_call_target="tpu_custom_call" | custom-call | tf_op jit(solution)/shard_map/pallas_call | solution.py:850
